TPU v7x, 32 devices: a whole 2x2x4 slice. The times are simulated.
32 devices in a mesh: tok: 8 (over z, x), col: 4 (over y, core).
Axes of the slice: x: 2, y: 2, z: 4, core: 2. Of those that a mesh axis runs over, the one named last changes fastest.
Arguments:
- tokens: bfloat16 [2560, 4096], P('tok', 'col'), may hold values from -16 to 16
- w_query: bfloat16 [4096, 2048], P(None, 'col'), may hold values from -0.09375 to 0.09375
- w_key: bfloat16 [4096, 512], P(None, 'col'), may hold values from -0.09375 to 0.09375
- w_value: bfloat16 [4096, 512], P(None, 'col'), may hold values from -0.09375 to 0.09375
- w_out: bfloat16 [2048, 4096], P('col'), may hold values from -0.125 to 0.125
- block_ids: int32 [16, 40, 16], P('col', 'tok'), may hold values from 0 to 39, as said below
- block_counts: int32 [16, 40], P('col', 'tok'), may hold values from 1 to 16, as said below
Outputs:
- mixed: bfloat16 [2560, 4096], P('tok', 'col')
Inputs may be any that keep to these rules, and one draw needn't show every extreme that they name: block_ids[h, b, 0] = b; the slots below block_counts[h, b] hold distinct blocks none after b; later slots hold block numbers that are not read. block_counts[h, b] <= b + 1; densities differ from head to head, and some row of some head uses all 16 slots.
All inputs are finite; a program needn't handle non-finite values.
Results may differ from a plain program's by a relative error of at most 0.012.
Values may be sent and summed in bfloat16 or wider, within the bound.
No kernel may reach another device: no remote copies, remote signals or barrier semaphores. Data moves between devices by JAX's collectives and lax.ppermute only.
A program may use at most 64 MiB of HBM per device.

v0:
```python
import jax
import jax.numpy as jnp
from jax import lax
from jax.sharding import PartitionSpec as P

HEAD_SIZE = 128
BLK = 64
NSEL = 16
rope_base = 500000.0


def rotate(field, positions):
    half = field.shape[-1] // 2
    freq = rope_base ** (-jnp.arange(half, dtype=jnp.float32) / half)
    angle = positions[:, None] * freq[None, :]
    cosine = jnp.cos(angle)[:, None, :]
    sine = jnp.sin(angle)[:, None, :]
    first = field[..., :half]
    second = field[..., half:]
    return jnp.concatenate(
        [first * cosine - second * sine, second * cosine + first * sine], axis=-1
    )


def on_device(tokens, w_query, w_key, w_value, w_out, block_ids, block_counts):
    tok_rows = tokens.shape[0]
    head_local = w_query.shape[1] // HEAD_SIZE
    kv_local = w_key.shape[1] // HEAD_SIZE
    group_size = head_local // kv_local
    blocks_dev = block_ids.shape[1]
    piece = lax.all_gather(tokens, "col", axis=1, tiled=True)
    width = piece.shape[1]

    def product(weight):
        return jnp.dot(piece, weight, preferred_element_type=jnp.float32)

    query_raw = product(w_query)
    key_raw = product(w_key)
    value_raw = product(w_value)
    tok_place = lax.axis_index("tok")
    query_index = tok_place * tok_rows + jnp.arange(tok_rows, dtype=jnp.int32)
    positions = query_index.astype(jnp.float32)
    query_rows = rotate(query_raw.reshape(tok_rows, head_local, HEAD_SIZE), positions).astype(
        jnp.bfloat16
    )
    keys = rotate(key_raw.reshape(tok_rows, kv_local, HEAD_SIZE), positions).astype(jnp.bfloat16)
    values = value_raw.astype(jnp.bfloat16).reshape(tok_rows, kv_local, HEAD_SIZE)
    grouped = query_rows.reshape(tok_rows, kv_local, group_size, HEAD_SIZE)
    live = jnp.arange(NSEL, dtype=jnp.int32)[None, None, :] < block_counts[:, :, None]
    last_query = tok_place * tok_rows + tok_rows - 1
    start_state = (
        jnp.full((head_local, tok_rows), -1e30, jnp.float32),
        jnp.zeros((head_local, tok_rows), jnp.float32),
        jnp.zeros((head_local, tok_rows, HEAD_SIZE), jnp.float32),
    )
    key_part = lax.all_gather(keys, "tok", axis=0, tiled=True)
    value_part = lax.all_gather(values, "tok", axis=0, tiled=True)
    amount = key_part.shape[0]
    width = 512
    key_blocks = key_part.reshape(amount // width, width, kv_local, HEAD_SIZE)
    value_blocks = value_part.reshape(amount // width, width, kv_local, HEAD_SIZE)
    offsets = jnp.arange(amount // width, dtype=jnp.int32) * width

    def one_block(state, inputs):
        key_block, value_block, offset = inputs

        def compute(inner_state):
            highest, total, summed_weights = inner_state
            key_index = offset + jnp.arange(width, dtype=jnp.int32)
            key_group = key_index // BLK
            hit = jnp.any(
                (block_ids[:, :, :, None] == key_group[None, None, None, :]) & live[..., None],
                axis=2,
            )
            allowed = jnp.broadcast_to(hit[:, :, None, :], (head_local, blocks_dev, BLK, width))
            allowed = allowed.reshape(head_local, tok_rows, width)
            allowed = allowed & (key_index[None, None, :] <= query_index[None, :, None])
            logit_scores = jnp.einsum(
                "tcgd,kcd->cgtk", grouped, key_block, preferred_element_type=jnp.float32
            )
            logit_scores = logit_scores.reshape(head_local, tok_rows, width) * HEAD_SIZE ** (-0.5)
            masked = jnp.where(allowed, logit_scores, -1e30)
            fresh = jnp.maximum(highest, jnp.max(masked, axis=-1))
            decay = jnp.exp(highest - fresh)
            weights = jnp.where(allowed, jnp.exp(masked - fresh[..., None]), 0.0)
            total = total * decay + jnp.sum(weights, axis=-1)
            rounded_scores = weights.astype(jnp.bfloat16).reshape(
                kv_local, group_size, tok_rows, width
            )
            added = jnp.einsum(
                "cgtk,kcd->cgtd", rounded_scores, value_block, preferred_element_type=jnp.float32
            )
            summed_weights = summed_weights * decay[..., None] + added.reshape(
                head_local, tok_rows, HEAD_SIZE
            )
            return (fresh, total, summed_weights)

        return (
            lax.cond(offset > last_query, lambda inner_state: inner_state, compute, state),
            None,
        )

    result, _ = lax.scan(one_block, start_state, (key_blocks, value_blocks, offsets))
    highest, total, summed_weights = result
    attended = jnp.transpose((summed_weights / total[..., None]).astype(jnp.bfloat16), (1, 0, 2))
    flat = attended.reshape(tok_rows, head_local * HEAD_SIZE)
    summed_out = lax.psum_scatter(
        lax.dot_general(
            w_out, flat, (((0,), (1,)), ((), ())), preferred_element_type=jnp.float32
        ).astype(jnp.bfloat16),
        "col",
        scatter_dimension=0,
        tiled=True,
    ).astype(jnp.float32)
    return jnp.transpose(summed_out).astype(jnp.bfloat16)


def solution(mesh):
    in_specs = (
        P("tok", "col"),
        P(None, "col"),
        P(None, "col"),
        P(None, "col"),
        P("col", None),
        P("col", "tok", None),
        P("col", "tok"),
    )
    out_specs = P("tok", "col")
    return jax.shard_map(
        on_device, mesh=mesh, in_specs=in_specs, out_specs=out_specs, check_vma=False
    )
```

profile of v0, /device:TPU:0, one launch (start us, length us, event | category | flops | bytes accessed | tf_op | source)
XLA Modules:
  0.0 185.4 jit_solution(4791514653528160586)
XLA Ops:
  6.5 0.7 all-gather.3.cloned.1.call-update
  7.3 0.7 copy.25
  8.0 0.6 multiply_cosine_fusion
  8.7 28.5 %all-gather.3.cloned.1.call-done = bf16[320,4096]{1,0:T(8,128)(2,1)} async-done(((bf16[320,1024]{1,0:T(8,128)(2,1)}), bf16[320,4096]{1,0:T(8,128)(2,1)}) %all-gather.3.cloned.1.call-update) | async-done | bytes 2621456 | tf_op jit(solution)/shard_map/all_gather | solution.py:31
  37.2 4.5 %fusion.43 = f32[320,512]{1,0:T(8,128)S(1)} fusion(bf16[320,4096]{1,0:T(8,128)(2,1)} %all-gather.3.cloned.1.call-done, bf16[4096,512]{1,0:T(8,128)(2,1)} %param.12), kind=kOutput, calls=%fused_computation.67 | convolution fusion | flops 1342177280 | bytes 7471104 | tf_op jit(solution)/shard_map/dot_general | solution.py:35
  41.7 0.2 reshape.338
  41.9 0.4 fusion.42
  42.3 1.3 copy-done.1
  43.7 0.8 convolution_bitcast_fusion
  44.5 0.7 fusion.39
  45.2 0.1 pad_maximum_fusion.1
  45.3 31.9 %all_gather.10 = bf16[2560,1,128]{2,0,1:T(8,128)(2,1)S(1)} all-gather(bf16[320,1,128]{2,0,1:T(8,128)(2,1)S(1)} %pad_maximum_fusion.1), channel_id=1, replica_groups=mesh['tok'=8,'col'=4] {'tok'}, dimensions={0}, use_global_device_ids=true | all-gather | bytes 737280 | tf_op jit(solution)/shard_map/all_gather | solution.py:56
  77.3 0.8 convolution_convert_fusion.1
  78.2 31.4 %all-gather = bf16[2560,128]{1,0:T(8,128)(2,1)S(1)} all-gather(bf16[320,128]{1,0:T(8,128)(2,1)S(1)} %convolution_convert_fusion.1), channel_id=2, replica_groups=mesh['tok'=8,'col'=4] {'tok'}, dimensions={0}, use_global_device_ids=true | all-gather | bytes 737280 | tf_op jit(solution)/shard_map/all_gather | solution.py:57
  109.6 0.2 fusion.29
  109.7 0.2 pad_maximum_fusion
  110.0 11.1 %while.15 = (s32[]{:T(128)}, f32[4,320]{1,0:T(4,128)S(1)}, f32[4,320]{1,0:T(4,128)S(1)}, f32[4,320,128]{2,1,0:T(8,128)S(1)}, s32[5]{0:T(128)S(1)}, /*index=5*/s3...) while((s32[]{:T(128)}, f32[4,320]{1,0:T(4,128)S(1)}, ...), condition=%wide.region_6.7_spmd.clone, body=%wide.region_0.6_spmd.clone.sunk | while | flops 347014272 | bytes 13164303 | solution.py:103
  110.0 0.6 dynamic_slice.33
  111.3 4.4 %conditional.3 = (f32[4,320]{1,0:T(4,128)S(1)}, f32[4,320]{1,0:T(4,128)S(1)}, f32[4,320,128]{2,1,0:T(8,128)S(1)}) conditional(s32[]{:T(128)} %convert_element_type.74, (s32[4,5,16]{2,1,0:T(8,128)S(1)}, s32[]{:T(128)}, s32[4,5,16]{2,1,0:T(8,128)S(1)}, s32[]{:T(128)}, bf16[5,512,1,128]{3,1,2,0:T(8,128)(2,1)S(1)}, /*index=5*/s32[]{:T(128)}, ...), branch_computations={%region_1.4_spmd, %region_5.5_spmd} | conditional | flops 347014272 | bytes 13151224 | solution.py:99
  111.3 0.6 add_select_fusion
  112.0 0.3 and_reduce_fusion
  112.3 0.2 broadcast_in_dim.4
  112.5 0.2 broadcast_compare_fusion
  112.7 0.8 fusion.4
  113.5 1.1 fusion.6
  114.6 1.0 fusion.11
  115.7 0.6 dynamic_slice.33
  117.0 0.6 dynamic_slice.33
  118.4 0.6 dynamic_slice.33
  119.7 0.6 dynamic_slice.33
  121.1 5.3 %fusion.28 = bf16[4096,320]{0,1:T(8,128)(2,1)} fusion(bf16[512,4096]{1,0:T(8,128)(2,1)} %param.15, f32[4,320,128]{2,1,0:T(8,128)S(1)} %get-tuple-element.165, f32[4,320]{1,0:T(4,128)S(1)} %get-tuple-element.166), kind=kOutput, calls=%fused_computation.38 | convolution fusion | flops 1343815680 | bytes 7476224 | tf_op jit(solution)/shard_map/dot_general | solution.py:108
  126.4 52.1 %reduce-scatter.2.cloned.1.call-done = bf16[1024,320]{0,1:T(8,128)(2,1)} async-done(((bf16[4096,320]{0,1:T(8,128)(2,1)}), bf16[1024,320]{0,1:T(8,128)(2,1)}) %reduce-scatter.2.cloned.1.call-update) | async-done | bytes 655376 | tf_op jit(solution)/shard_map/reduce_scatter | solution.py:107
  (43 shorter events, 0.4 us)
Async XLA Ops:
  6.5 35.8 %copy-start = (bf16[4096,128]{1,0:T(8,128)(2,1)S(1)}, bf16[4096,128]{1,0:T(8,128)(2,1)}, u32[]{:S(2)}) copy-start(bf16[4096,128]{1,0:T(8,128)(2,1)} %param.13) | copy-start | bytes 3145732
  6.5 30.6 %all-gather.3.cloned.1.call-start = ((), (), s32[]{:S(2)}) async-start(), calls=%async_computation.1 | async-start | bytes 3276800 | tf_op jit(solution)/shard_map/all_gather | solution.py:31
  7.3 171.3 %reduce-scatter.2.cloned.1.call-start = ((), (), s32[]{:S(2)}) async-start(), calls=%async_computation.2 | async-start | bytes 3276800 | tf_op jit(solution)/shard_map/reduce_scatter | solution.py:107
  41.9 1.7 copy-start.1
  43.7 33.6 %copy-start.2 = (bf16[4096,128]{1,0:T(8,128)(2,1)S(1)}, bf16[4096,128]{1,0:T(8,128)(2,1)}, u32[]{:S(2)}) copy-start(bf16[4096,128]{1,0:T(8,128)(2,1)} %param.14) | copy-start | bytes 3145732
  78.1 31.9 %copy-start.3 = (s32[4,5]{1,0:T(4,128)S(1)}, s32[4,5]{1,0:T(4,128)}, u32[]{:S(2)}) copy-start(s32[4,5]{1,0:T(4,128)} %param.17) | copy-start | bytes 244
Sparse Core Ops, SparseCore 0:
  8.9 28.2 all-gather.2
  126.5 51.9 reduce-scatter.1
where the time goes:
time: 186 us; the launch traced here: 185 us
  waiting for transfers between devices  81.4 us (44%)
  blocking collectives  63.3 us (34%)
  between operations  13.5 us (7%)
  matrix products  13.4 us (7%)
  local copies, waits for them, and re-layouts  6.13 us (3%)
  other arithmetic  4.08 us (2%)
  loops' own time  3.5 us (2%)
    reduce_scatter x1, waiting for transfers between devices, on_device(): lax.psum_scatter(lax.dot_general(w_out, flat, (((0,), (1,)), ((), ())), p...  52.1 us
    all_gather x1, blocking collectives, on_device(): key_part = lax.all_gather(keys, 'tok', axis=0, tiled=True)  31.9 us
    all_gather x1, blocking collectives, on_device(): value_part = lax.all_gather(values, 'tok', axis=0, tiled=True)  31.4 us
    all_gather x1, waiting for transfers between devices, on_device(): piece = lax.all_gather(tokens, 'col', axis=1, tiled=True)  28.5 us
    dot_general x3, matrix products, product(): return jnp.dot(piece, weight, preferred_element_type=jnp.float32)  6.19 us
    dot_general x1, matrix products, on_device(): lax.dot_general(w_out, flat, (((0,), (1,)), ((), ())), preferred_element_...  5.31 us
  transfers between devices with their start and end apart: 2, of which 2 were waited for; matrix products, arithmetic and copies ran while one was open for 1% of the time, Pallas kernels for 0%

commit v1 on v0

--- a/solution.py
+++ b/solution.py
@@ -7,6 +7,24 @@
 BLK = 64
 NSEL = 16
 rope_base = 500000.0
+
+
+def laid_out(blocks, dim):
+    shape = list(blocks.shape[1:])
+    shape[dim] *= blocks.shape[0]
+    return jnp.moveaxis(blocks, 0, dim).reshape(shape)
+
+
+def collected_by_bits(x, axis):
+    size = lax.axis_size(axis)
+    blocks = x[None]
+    for level in range(size.bit_length() - 1):
+        bit = 1 << level
+        other = lax.ppermute(blocks, axis, [(i, i ^ bit) for i in range(size)])
+        both = jnp.stack([blocks, other])
+        upper = lax.axis_index(axis) >> level & 1
+        blocks = jnp.where(upper == 0, both, both[::-1]).reshape(-1, *x.shape)
+    return blocks
 
 
 def rotate(field, positions):
@@ -53,7 +71,7 @@
         jnp.zeros((head_local, tok_rows), jnp.float32),
         jnp.zeros((head_local, tok_rows, HEAD_SIZE), jnp.float32),
     )
-    key_part = lax.all_gather(keys, "tok", axis=0, tiled=True)
+    key_part = laid_out(collected_by_bits(keys, "tok"), 0)
     value_part = lax.all_gather(values, "tok", axis=0, tiled=True)
     amount = key_part.shape[0]
     width = 512

time: 186 us -> 170 us (0.914)
  blocking collectives: 63.3 us -> 37 us
  starting transfers between devices: 0.04 us -> 5.59 us
  matrix products: 13.4 us -> 17.1 us
    all_gather x1 -> x0, blocking collectives: 31.9 us -> none  [on_device(): key_part = lax.all_gather(keys, 'tok', axis=0, tiled=True)]
    all_gather x1, blocking collectives: 31.4 us -> 37 us  [on_device(): value_part = lax.all_gather(values, 'tok', axis=0, tiled=True)]
    ppermute x0 -> x3, starting transfers between devices: none -> 5.55 us  [collected_by_bits(): other = lax.ppermute(blocks, axis, [(i, i ^ bit) for i in range(size)])]
    ppermute x0 -> x3, waiting for transfers between devices: none -> 4.4 us  [collected_by_bits(): other = lax.ppermute(blocks, axis, [(i, i ^ bit) for i in range(size)])]
    dot_general x3, matrix products: 6.19 us -> 9.89 us  [product(): return jnp.dot(piece, weight, preferred_element_type=jnp.float32)]
    reduce_scatter x1, waiting for transfers between devices: 52.1 us -> 49 us  [on_device(): lax.psum_scatter(lax.dot_general(w_out, flat, (((0,), (1,)), ((), ())), p...]
  transfers between devices with their start and end apart: 2 -> 5, of which waited for: 2 -> 3; matrix products, arithmetic and copies ran while one was open for 1% -> 6% of each run, Pallas kernels for 0% -> 0%
where the time goes in v1:
time: 170 us
  waiting for transfers between devices  82.6 us (49%)
  blocking collectives  37 us (22%)
  matrix products  17.1 us (10%)
  between operations  13.6 us (8%)
  local copies, waits for them, and re-layouts  5.64 us (3%)
  starting transfers between devices  5.59 us (3%)
  other arithmetic  4.54 us (3%)
  loops' own time  3.61 us (2%)
    reduce_scatter x1, waiting for transfers between devices, on_device(): lax.psum_scatter(lax.dot_general(w_out, flat, (((0,), (1,)), ((), ())), p...  49 us
    all_gather x1, blocking collectives, on_device(): value_part = lax.all_gather(values, 'tok', axis=0, tiled=True)  37 us
    all_gather x1, waiting for transfers between devices, on_device(): piece = lax.all_gather(tokens, 'col', axis=1, tiled=True)  28.5 us
    dot_general x3, matrix products, product(): return jnp.dot(piece, weight, preferred_element_type=jnp.float32)  9.89 us
    ppermute x3, starting transfers between devices, collected_by_bits(): other = lax.ppermute(blocks, axis, [(i, i ^ bit) for i in range(size)])  5.55 us
    dot_general x1, matrix products, on_device(): lax.dot_general(w_out, flat, (((0,), (1,)), ((), ())), preferred_element_...  5.31 us
    ppermute x3, waiting for transfers between devices, collected_by_bits(): other = lax.ppermute(blocks, axis, [(i, i ^ bit) for i in range(size)])  4.4 us
    another operation x1, loops' own time, on_device(): lax.scan(one_block, start_state, (key_blocks, value_blocks, offsets))  3.44 us
  transfers between devices with their start and end apart: 5, of which 3 were waited for; matrix products, arithmetic and copies ran while one was open for 6% of the time, Pallas kernels for 0%

profile of v1, /device:TPU:0, one launch (start us, length us, event | category | flops | bytes accessed | tf_op | source)
XLA Modules:
  0.0 169.6 jit_solution(1893614936240478748)
XLA Ops:
  6.5 0.7 all-gather.3.cloned.1.call-update
  7.3 0.7 copy.23
  8.1 0.6 multiply_cosine_fusion
  8.7 28.5 %all-gather.3.cloned.1.call-done = bf16[320,4096]{1,0:T(8,128)(2,1)} async-done(((bf16[320,1024]{1,0:T(8,128)(2,1)}), bf16[320,4096]{1,0:T(8,128)(2,1)}) %all-gather.3.cloned.1.call-update) | async-done | bytes 2621456 | tf_op jit(solution)/shard_map/all_gather | solution.py:49
  37.2 2.7 %convolution_bitcast_fusion = f32[320,1,128]{2,0,1:T(8,128)S(1)} fusion(bf16[320,4096]{1,0:T(8,128)(2,1)} %all-gather.3.cloned.1.call-done, bf16[4096,128]{1,0:T(8,128)(2,1)S(1)} %copy-done), kind=kOutput, calls=%fused_computation.39 | convolution fusion | flops 335544320 | bytes 3833856 | tf_op jit(solution)/shard_map/dot_general | solution.py:53
  39.9 0.7 fusion.39
  40.8 1.5 collective-permute-start
  42.3 4.6 %fusion.45 = f32[320,512]{1,0:T(8,128)} fusion(bf16[320,4096]{1,0:T(8,128)(2,1)S(1)} %copy-done.1, bf16[4096,512]{1,0:T(8,128)(2,1)} %param.12), kind=kOutput, calls=%fused_computation.75 | convolution fusion | flops 1342177280 | bytes 7471104 | tf_op jit(solution)/shard_map/dot_general | solution.py:53
  46.9 1.3 reshape.385
  48.2 2.6 %convolution_convert_fusion.1 = bf16[320,128]{1,0:T(8,128)(2,1)S(1)} fusion(bf16[320,4096]{1,0:T(8,128)(2,1)} %all-gather.3.cloned.1.call-done, bf16[4096,128]{1,0:T(8,128)(2,1)S(1)} %copy-done.2), kind=kOutput, calls=%fused_computation.40 | convolution fusion | flops 335585280 | bytes 3751936 | tf_op jit(solution)/shard_map/dot_general | solution.py:53
  50.8 0.4 fusion.44
  51.3 1.6 collective-permute-start.1
  52.9 0.2 fusion.29
  53.1 4.4 %collective-permute-done.1 = bf16[2,320,1,128]{3,1,0,2:T(8,128)(2,1)S(1)} collective-permute-done((bf16[2,320,1,128]{3,1,0,2:T(8,128)(2,1)S(1)}, bf16[2,320,1,128]{3,1,0,2:T(8,128)(2,1)S(1)}, u32[]{:S(2)}, u32[]{:S(2)}) %collective-permute-start.1) | collective-permute-done | bytes 163872 | tf_op jit(solution)/shard_map/ppermute | solution.py:23
  57.6 2.5 %collective-permute-start.2 = (bf16[4,320,1,128]{3,1,0,2:T(8,128)(2,1)S(1)}, bf16[4,320,1,128]{3,1,0,2:T(8,128)(2,1)S(1)}, u32[]{:S(2)}, u32[]{:S(2)}) collective-permute-start(bf16[4,320,1,128]{3,1,0,2:T(8,128)(2,1)S(1)} %bitcast.88), channel_id=1, source_target_pairs={{0,16},{4,20},{8,24},{12,28},{16,0},{20,4},{24,8},{28,12},{1,17},{... | collective-permute-start | bytes 983048 | tf_op jit(solution)/shard_map/ppermute | solution.py:23
  60.1 0.2 pad_maximum_fusion.2
  60.2 37.0 %all-gather = bf16[2560,128]{1,0:T(8,128)(2,1)S(1)} all-gather(bf16[320,128]{1,0:T(8,128)(2,1)S(1)} %convolution_convert_fusion.1), channel_id=2, replica_groups=mesh['tok'=8,'col'=4] {'tok'}, dimensions={0}, use_global_device_ids=true | all-gather | bytes 737280 | tf_op jit(solution)/shard_map/all_gather | solution.py:75
  97.6 10.9 %while.15 = (s32[]{:T(128)}, f32[4,320]{1,0:T(4,128)S(1)}, f32[4,320]{1,0:T(4,128)S(1)}, f32[4,320,128]{2,1,0:T(8,128)S(1)}, s32[5]{0:T(128)S(1)}, /*index=5*/s3...) while((s32[]{:T(128)}, f32[4,320]{1,0:T(4,128)S(1)}, ...), condition=%wide.region_6.7_spmd.clone, body=%wide.region_0.6_spmd.clone.sunk | while | flops 347014272 | bytes 13164303 | solution.py:121
  97.6 0.6 dynamic_slice.33
  98.8 4.4 %conditional.3 = (f32[4,320]{1,0:T(4,128)S(1)}, f32[4,320]{1,0:T(4,128)S(1)}, f32[4,320,128]{2,1,0:T(8,128)S(1)}) conditional(s32[]{:T(128)} %convert_element_type.82, (s32[4,5,16]{2,1,0:T(8,128)S(1)}, s32[]{:T(128)}, s32[4,5,16]{2,1,0:T(8,128)S(1)}, s32[]{:T(128)}, bf16[5,512,1,128]{3,1,2,0:T(8,128)(2,1)S(1)}, /*index=5*/s32[]{:T(128)}, ...), branch_computations={%region_1.4_spmd, %region_5.5_spmd} | conditional | flops 347014272 | bytes 13151224 | solution.py:117
  98.8 0.7 add_select_fusion
  99.6 0.3 and_reduce_fusion
  99.8 0.2 broadcast_in_dim.4
  100.2 0.8 fusion.4
  101.0 1.1 fusion.6
  102.2 1.0 fusion.11
  103.3 0.6 dynamic_slice.33
  104.6 0.6 dynamic_slice.33
  105.9 0.6 dynamic_slice.33
  107.2 0.6 dynamic_slice.33
  108.5 5.3 %fusion.28 = bf16[4096,320]{0,1:T(8,128)(2,1)} fusion(bf16[512,4096]{1,0:T(8,128)(2,1)} %param.15, f32[4,320,128]{2,1,0:T(8,128)S(1)} %get-tuple-element.165, f32[4,320]{1,0:T(4,128)S(1)} %get-tuple-element.166), kind=kOutput, calls=%fused_computation.38 | convolution fusion | flops 1343815680 | bytes 7476224 | tf_op jit(solution)/shard_map/dot_general | solution.py:126
  113.8 49.0 %reduce-scatter.2.cloned.1.call-done = bf16[1024,320]{0,1:T(8,128)(2,1)} async-done(((bf16[4096,320]{0,1:T(8,128)(2,1)}), bf16[1024,320]{0,1:T(8,128)(2,1)}) %reduce-scatter.2.cloned.1.call-update) | async-done | bytes 655376 | tf_op jit(solution)/shard_map/reduce_scatter | solution.py:125
  (54 shorter events, 1.1 us)
Async XLA Ops:
  6.5 30.7 %copy-start = (bf16[4096,128]{1,0:T(8,128)(2,1)S(1)}, bf16[4096,128]{1,0:T(8,128)(2,1)}, u32[]{:S(2)}) copy-start(bf16[4096,128]{1,0:T(8,128)(2,1)} %param.13) | copy-start | bytes 3145732
  6.5 30.6 %all-gather.3.cloned.1.call-start = ((), (), s32[]{:S(2)}) async-start(), calls=%async_computation.1 | async-start | bytes 3276800 | tf_op jit(solution)/shard_map/all_gather | solution.py:49
  7.3 155.5 %reduce-scatter.2.cloned.1.call-start = ((), (), s32[]{:S(2)}) async-start(), calls=%async_computation.2 | async-start | bytes 3276800 | tf_op jit(solution)/shard_map/reduce_scatter | solution.py:125
  37.2 5.1 %copy-start.1 = (bf16[320,4096]{1,0:T(8,128)(2,1)S(1)}, bf16[320,4096]{1,0:T(8,128)(2,1)}, u32[]{:S(2)}) copy-start(bf16[320,4096]{1,0:T(8,128)(2,1)} %all-gather.3.cloned.1.call-done) | copy-start | bytes 7864324
  40.7 7.4 %copy-start.2 = (bf16[4096,128]{1,0:T(8,128)(2,1)S(1)}, bf16[4096,128]{1,0:T(8,128)(2,1)}, u32[]{:S(2)}) copy-start(bf16[4096,128]{1,0:T(8,128)(2,1)} %param.14) | copy-start | bytes 3145732
  40.8 10.4 %collective-permute-start = (bf16[1,320,1,128]{3,1,2,0:T(8,128)(2,1)S(1)}, bf16[1,320,1,128]{3,1,2,0:T(8,128)(2,1)S(1)}, u32[]{:S(2)}, u32[]{:S(2)}) collective-permute-start(bf16[1,320,1,128]{3,1,2,0:T(8,128)(2,1)S(1)} %pad_maximum_fusion.4), channel_id=1, source_target_pairs={{0,4},{4,0},{8,12},{12,8},{16,20},{20,16},{24,28},{28,24},{1,5},{5... | collective-permute-start | bytes 245768 | tf_op jit(solution)/shard_map/ppermute | solution.py:23
  51.3 6.1 %collective-permute-start.1 = (bf16[2,320,1,128]{3,1,0,2:T(8,128)(2,1)S(1)}, bf16[2,320,1,128]{3,1,0,2:T(8,128)(2,1)S(1)}, u32[]{:S(2)}, u32[]{:S(2)}) collective-permute-start(bf16[2,320,1,128]{3,1,0,2:T(8,128)(2,1)S(1)} %get-tuple-element.278), channel_id=1, source_target_pairs={{0,8},{4,12},{8,0},{12,4},{16,24},{20,28},{24,16},{28,20},{1,9},{5... | collective-permute-start | bytes 491528 | tf_op jit(solution)/shard_map/ppermute | solution.py:23
  57.6 40.0 %copy-start.3 = (s32[4,5]{1,0:T(4,128)S(1)}, s32[4,5]{1,0:T(4,128)}, u32[]{:S(2)}) copy-start(s32[4,5]{1,0:T(4,128)} %param.17) | copy-start | bytes 244
  57.6 39.7 %collective-permute-start.2 = (bf16[4,320,1,128]{3,1,0,2:T(8,128)(2,1)S(1)}, bf16[4,320,1,128]{3,1,0,2:T(8,128)(2,1)S(1)}, u32[]{:S(2)}, u32[]{:S(2)}) collective-permute-start(bf16[4,320,1,128]{3,1,0,2:T(8,128)(2,1)S(1)} %bitcast.88), channel_id=1, source_target_pairs={{0,16},{4,20},{8,24},{12,28},{16,0},{20,4},{24,8},{28,12},{1,17},{... | collective-permute-start | bytes 983048 | tf_op jit(solution)/shard_map/ppermute | solution.py:23
Sparse Core Ops, SparseCore 0:
  8.9 28.2 all-gather.2
  113.9 48.7 reduce-scatter.1
